TPU v7x, 512 devices: a whole 4x4x16 slice. The times are simulated.
512 devices in a mesh: gx: 32 (over y, x, z_hi), gy: 8 (over z_lo), gz: 2 (over core).
Axes of the slice: x: 4, y: 4, z: 16 (z_hi: 2, z_lo: 8; z = z_hi * 8 + z_lo), core: 2. Of those that a mesh axis runs over, the one named last changes fastest.
Arguments:
- source: float32 [256, 64, 4096], P('gx', 'gz', 'gy'), may hold values from -24 to 24
- coef: float32 [256, 64, 128], P('gx', 'gz', 'gy'), may hold values from 0.01 to 0.05
- face_trace: int32 [256, 2, 128], P('gx', 'gz'), may hold values from 0 to 1023, as said below
- near_col: int32 [32, 2, 8], P('gx', 'gz', 'gy'), may hold values from 0 to 63, as said below
- far_col: int32 [32, 2, 8, 7], P('gx', 'gz', 'gy'), may hold values from 0 to 63, as said below
- near_tile: bfloat16 [32, 2, 8, 1024, 1024], P('gx', 'gz', 'gy'), may hold values from -0.1875 to 0.1875
- far_u: bfloat16 [32, 2, 8, 7, 16, 1024], P('gx', 'gz', 'gy'), may hold values from -0.1875 to 0.1875
- far_v: bfloat16 [32, 2, 8, 7, 16, 1024], P('gx', 'gz', 'gy'), may hold values from -0.1875 to 0.1875
Outputs:
- solution: float32 [256, 64, 4096], P('gx', 'gz', 'gy')
- flux: float32 [256, 2, 4096], P('gx', 'gz', 'gy')
Inputs may be any that keep to these rules, and one draw needn't show every extreme that they name: For every block of 8 rows of x and each face s, the entries face_trace(x, s, y) of that block are a permutation of 0 to 1023. For every row block, near_col over the slots j together with far_col over j and k name each column block 0 to 63 exactly once. `far_col`: see near_col: near and far column blocks of a row block together name every column block exactly once.
All inputs are finite; a program needn't handle non-finite values.
Results may differ from a plain program's by a relative error of at most 0.003.
Values may be sent and summed in bfloat16 or wider, within the bound.
A program may use at most 64 MiB of HBM per device.

v0:
```python
import jax
import jax.numpy as jnp
from jax import lax
from jax.sharding import PartitionSpec as P

E = 32
SWEEPS = 3


def extended(block, sides, width):
    for axis, dim in sides:
        count = lax.axis_size(axis)
        forward = [(i, i + 1) for i in range(count - 1)]
        backward = [(target, source) for source, target in forward]
        low = lax.ppermute(
            lax.slice_in_dim(block, block.shape[dim] - width, None, axis=dim), axis, forward
        )
        high = lax.ppermute(lax.slice_in_dim(block, 0, width, axis=dim), axis, backward)
        block = jnp.concatenate([low, block, high], axis=dim)
    return block


def sweep(field, rhs, diag):
    slab = extended(field, (("gx", 0), ("gz", 1)), 1)
    pencil = extended(field, (("gy", 2),), E)
    beside = slab[2:, 1:-1] + slab[:-2, 1:-1] + slab[1:-1, 2:] + slab[1:-1, :-2]
    beside = beside + pencil[:, :, 2 * E :] + pencil[:, :, : -2 * E]
    return (rhs + beside) / diag


def body(source, coef, face_trace, near_col, far_col, near_tile, far_u, far_v):
    rows_x = source.shape[0]
    depth = source.shape[1]
    cells_y = coef.shape[2]
    groups = lax.axis_size("gy")
    mine_y = lax.axis_index("gy")
    face_side = lax.axis_index("gz")
    tile = near_tile.shape[3]
    far_count = far_u.shape[3]
    rank = far_u.shape[4]
    diag = jnp.repeat(6.0 + coef, E, axis=2)
    field = jnp.zeros(source.shape, jnp.float32)
    for step in range(SWEEPS):
        field = sweep(field, source, diag)
    plane = jnp.where(face_side == 0, 0, depth - 1)
    depth_ids = jnp.arange(depth, dtype=jnp.int32)
    plane_mask = (depth_ids == plane).astype(jnp.float32)
    face_local = jnp.where(face_side == 0, field[:, 0, :], field[:, depth - 1, :]).astype(
        jnp.bfloat16
    )
    face_block = lax.all_gather(face_local, "gy", axis=1, tiled=True)
    perm = face_trace.reshape(tile)
    inverse = jnp.zeros((tile,), jnp.int32).at[perm].set(jnp.arange(tile, dtype=jnp.int32))
    block_traces = face_block.reshape(tile, E)[inverse].T
    wanted = jnp.concatenate([near_col.reshape(1), far_col.reshape(far_count)])
    piece = lax.all_gather(block_traces[None], ("gx", "gz"), axis=0, tiled=True)
    numbers = jnp.arange(piece.shape[0], dtype=jnp.int32)
    onehot = (wanted[:, None] == numbers[None, :]).astype(jnp.bfloat16)
    chosen = jnp.einsum("cn,net->cet", onehot, piece, preferred_element_type=jnp.float32).astype(
        jnp.bfloat16
    )
    nearpart = lax.dot_general(
        chosen[0],
        near_tile.reshape(tile, tile),
        (((1,), (1,)), ((), ())),
        preferred_element_type=jnp.float32,
    )
    weights = jnp.einsum(
        "fet,frt->fer",
        chosen[1:],
        far_v.reshape(far_count, rank, tile),
        preferred_element_type=jnp.float32,
    ).astype(jnp.bfloat16)
    farpart = jnp.einsum(
        "fer,frt->et",
        weights,
        far_u.reshape(far_count, rank, tile),
        preferred_element_type=jnp.float32,
    )
    partial_rows = nearpart + farpart
    total = lax.psum(partial_rows, "gy")
    face_flux = total[:, perm].reshape(E, rows_x, cells_y * groups)
    mine = lax.dynamic_slice_in_dim(face_flux, mine_y * cells_y, cells_y, 2)
    flux_rows = mine.transpose(1, 2, 0).reshape(rows_x, cells_y * E)
    extra = plane_mask[None, :, None] * flux_rows[:, None, :]
    solution = sweep(field, source + extra, diag)
    return (solution, flux_rows[:, None, :])


def solution(mesh):
    return jax.shard_map(
        body,
        mesh=mesh,
        in_specs=(
            P("gx", "gz", "gy"),
            P("gx", "gz", "gy"),
            P("gx", "gz", None),
            P("gx", "gz", "gy"),
            P("gx", "gz", "gy", None),
            P("gx", "gz", "gy", None, None),
            P("gx", "gz", "gy", None, None, None),
            P("gx", "gz", "gy", None, None, None),
        ),
        out_specs=(P("gx", "gz", "gy"), P("gx", "gz", "gy")),
        check_vma=False,
    )
```

profile of v0, /device:TPU:2, one launch (start us, length us, event | category | flops | bytes accessed | tf_op | source)
XLA Modules:
  0.0 448.9 jit_solution(9452833639911425397)
XLA Ops:
  7.2 15.8 %collective-permute-start = (f32[1,32,512]{2,1,0:T(8,128)S(1)}, f32[1,32,512]{2,1,0:T(8,128)S(1)}, u32[]{:S(2)}, u32[]{:S(2)}) collective-permute-start(f32[1,32,512]{2,1,0:T(8,128)S(1)} %broadcast.45), channel_id=1, source_target_pairs={{16,0},{32,16},{48,32},{64,48},{80,64},{96,80},{112,96},{128,112},... | collective-permute-start | bytes 196616 | tf_op jit(solution)/shard_map/ppermute | solution.py:18
  23.1 1.9 collective-permute-start.1
  25.7 1.3 collective-permute-start.4
  27.0 5.2 %collective-permute-start.5 = (f32[8,32,32]{2,1,0:T(8,128)}, f32[8,32,32]{2,1,0:T(8,128)}, u32[]{:S(2)}, u32[]{:S(2)}) collective-permute-start(f32[8,32,32]{2,1,0:T(8,128)} %broadcast.46), channel_id=1, source_target_pairs={{0,2},{2,4},{4,6},{6,8},{8,10},{10,12},{12,14},{1,3},{3,5},{5,7},{... | collective-permute-start | bytes 98312 | tf_op jit(solution)/shard_map/ppermute | solution.py:15
  32.2 7.6 %collective-permute-done.1 = f32[1,32,512]{2,1,0:T(8,128)S(1)} collective-permute-done((f32[1,32,512]{2,1,0:T(8,128)S(1)}, f32[1,32,512]{2,1,0:T(8,128)S(1)}, u32[]{:S(2)}, u32[]{:S(2)}) %collective-permute-start.1) | collective-permute-done | bytes 65568 | tf_op jit(solution)/shard_map/ppermute | solution.py:15
  39.9 1.3 collective-permute-start.2
  41.2 3.0 collective-permute-start.3
  44.2 0.8 broadcast_add_fusion
  45.2 2.0 broadcast_in_dim.18
  47.2 2.3 reshape.71
  49.5 1.6 fusion.14
  51.2 5.9 %collective-permute-start.6 = (f32[1,32,512]{2,1,0:T(8,128)S(1)}, f32[1,32,512]{2,1,0:T(8,128)S(1)}, u32[]{:S(2)}, u32[]{:S(2)}) collective-permute-start(f32[1,32,512]{2,1,0:T(8,128)S(1)} %get-tuple-element.19), channel_id=1, source_target_pairs={{16,0},{32,16},{48,32},{64,48},{80,64},{96,80},{112,96},{128,112},... | collective-permute-start | bytes 196616 | tf_op jit(solution)/shard_map/ppermute | solution.py:18
  57.1 8.6 %collective-permute-start.7 = (f32[1,32,512]{2,1,0:T(8,128)S(1)}, f32[1,32,512]{2,1,0:T(8,128)S(1)}, u32[]{:S(2)}, u32[]{:S(2)}) collective-permute-start(f32[1,32,512]{2,1,0:T(8,128)S(1)} %get-tuple-element.18), channel_id=1, source_target_pairs={{0,16},{16,32},{32,48},{48,64},{64,80},{80,96},{96,112},{112,128},... | collective-permute-start | bytes 196616 | tf_op jit(solution)/shard_map/ppermute | solution.py:15
  66.5 1.3 collective-permute-start.10
  67.8 6.8 %collective-permute-start.11 = (f32[8,32,32]{2,1,0:T(8,128)}, f32[8,32,32]{2,1,0:T(8,128)S(1)}, u32[]{:S(2)}, u32[]{:S(2)}) collective-permute-start(f32[8,32,32]{2,1,0:T(8,128)} %get-tuple-element.21), channel_id=1, source_target_pairs={{0,2},{2,4},{4,6},{6,8},{8,10},{10,12},{12,14},{1,3},{3,5},{5,7},{... | collective-permute-start | bytes 98312 | tf_op jit(solution)/shard_map/ppermute | solution.py:15
  75.2 1.3 collective-permute-start.8
  76.5 4.2 collective-permute-start.9
  81.4 4.3 scatter_custom_fusion
  85.8 2.9 fusion.31
  88.7 4.6 %collective-permute-start.12 = (f32[1,32,512]{2,1,0:T(8,128)S(1)}, f32[1,32,512]{2,1,0:T(8,128)S(1)}, u32[]{:S(2)}, u32[]{:S(2)}) collective-permute-start(f32[1,32,512]{2,1,0:T(8,128)S(1)} %get-tuple-element.15), channel_id=1, source_target_pairs={{16,0},{32,16},{48,32},{64,48},{80,64},{96,80},{112,96},{128,112},... | collective-permute-start | bytes 196616 | tf_op jit(solution)/shard_map/ppermute | solution.py:18
  93.3 9.9 %collective-permute-start.13 = (f32[1,32,512]{2,1,0:T(8,128)S(1)}, f32[1,32,512]{2,1,0:T(8,128)S(1)}, u32[]{:S(2)}, u32[]{:S(2)}) collective-permute-start(f32[1,32,512]{2,1,0:T(8,128)S(1)} %get-tuple-element.14), channel_id=1, source_target_pairs={{0,16},{16,32},{32,48},{48,64},{64,80},{80,96},{96,112},{112,128},... | collective-permute-start | bytes 196616 | tf_op jit(solution)/shard_map/ppermute | solution.py:15
  104.0 1.3 collective-permute-start.16
  105.3 6.3 %collective-permute-start.17 = (f32[8,32,32]{2,1,0:T(8,128)}, f32[8,32,32]{2,1,0:T(8,128)S(1)}, u32[]{:S(2)}, u32[]{:S(2)}) collective-permute-start(f32[8,32,32]{2,1,0:T(8,128)} %get-tuple-element.17), channel_id=1, source_target_pairs={{0,2},{2,4},{4,6},{6,8},{8,10},{10,12},{12,14},{1,3},{3,5},{5,7},{... | collective-permute-start | bytes 98312 | tf_op jit(solution)/shard_map/ppermute | solution.py:15
  112.3 1.3 collective-permute-start.14
  113.6 4.2 collective-permute-start.15
  118.4 2.9 fusion.24
  121.3 0.8 copy-done.2
  122.1 42.9 %all-gather = bf16[8,1,4096]{2,1,0:T(2,128)(2,1)S(1)} all-gather(bf16[8,1,512]{2,1,0:T(2,128)(2,1)S(1)} %fusion.43), channel_id=2, replica_groups=mesh['gx'=32,'gy'=8,'gz'=2] {'gy'}, dimensions={2}, use_global_device_ids=true | all-gather | bytes 73728 | tf_op jit(solution)/shard_map/all_gather | solution.py:51
  165.5 4.3 gather_fusion
  169.8 1.7 copy.17
  172.4 1.5 fusion.50
  173.9 3.7 collective-permute-start.18
  177.6 11.0 %collective-permute-start.19 = (f32[1,32,512]{2,1,0:T(8,128)}, f32[1,32,512]{2,1,0:T(8,128)S(1)}, u32[]{:S(2)}, u32[]{:S(2)}) collective-permute-start(f32[1,32,512]{2,1,0:T(8,128)} %get-tuple-element.10), channel_id=1, source_target_pairs={{0,16},{16,32},{32,48},{48,64},{64,80},{80,96},{96,112},{112,128},... | collective-permute-start | bytes 196616 | tf_op jit(solution)/shard_map/ppermute | solution.py:15
  188.6 117.6 %all-gather.4.cloned.1.call-done = bf16[2048,1024]{1,0:T(8,128)(2,1)} async-done(((bf16[32,1024]{1,0:T(8,128)(2,1)}), bf16[2048,1024]{1,0:T(8,128)(2,1)}) %all-gather.4.cloned.1.call-update) | async-done | bytes 4194320 | tf_op jit(solution)/shard_map/all_gather | solution.py:56
  306.2 6.7 %fusion.4 = bf16[8,32,1024]{2,0,1:T(8,128)(2,1)S(1)} fusion(bf16[64,32,1024]{2,1,0:T(8,128)(2,1)} %bitcast.35, s32[8]{0:T(128)S(1)} %pad_add_fusion), kind=kOutput, calls=%fused_computation.7 | convolution fusion | flops 33817088 | bytes 4718624 | tf_op jit(solution)/shard_map/cn,net->cet/dot_general | solution.py:59
  312.9 0.9 slice.231
  314.6 2.5 fusion.7
  317.2 1.7 fusion.51
  318.9 1.3 collective-permute-start.22
  320.2 5.2 %collective-permute-start.23 = (f32[8,32,32]{2,1,0:T(8,128)}, f32[8,32,32]{2,1,0:T(8,128)}, u32[]{:S(2)}, u32[]{:S(2)}) collective-permute-start(f32[8,32,32]{2,1,0:T(8,128)} %get-tuple-element.13), channel_id=1, source_target_pairs={{0,2},{2,4},{4,6},{6,8},{8,10},{10,12},{12,14},{1,3},{3,5},{5,7},{... | collective-permute-start | bytes 98312 | tf_op jit(solution)/shard_map/ppermute | solution.py:15
  325.4 1.6 pad_maximum_fusion.38
  327.0 1.3 collective-permute-start.20
  328.3 3.0 collective-permute-start.21
  331.3 98.3 %all-reduce.6.cloned.1.call-done = f32[32,1024]{1,0:T(8,128)} async-done(((f32[32,1024]{1,0:T(8,128)}), f32[32,1024]{1,0:T(8,128)}) %all-reduce.6.cloned.1.call-update) | async-done | bytes 131088 | tf_op jit(solution)/shard_map/psum | solution.py:81
  429.7 1.9 copy.20
  431.6 5.0 %gather_fusion.1 = f32[1024,32]{1,0:T(8,128)} fusion(f32[32,1024]{0,1:T(8,128)} %copy.20, s32[1024]{0:T(1024)S(1)} %broadcast_clamp_fusion), kind=kCustom, calls=%fused_computation.1 | custom fusion | bytes 266240 | tf_op jit(solution)/shard_map/gather | solution.py:82
  436.6 0.8 dynamic-slice_bitcast_fusion
  438.3 3.8 fusion.17
  (64 shorter events, 7.4 us)
Async XLA Ops:
  7.2 306.7 %copy-start = (bf16[1,1,1,1024,1024]{4,3,2,1,0:T(8,128)(2,1)S(1)}, bf16[1,1,1,1024,1024]{4,3,2,1,0:T(8,128)(2,1)}, u32[]{:S(2)}) copy-start(bf16[1,1,1,1024,1024]{4,3,2,1,0:T(8,128)(2,1)} %param.13) | copy-start | bytes 6291460
  7.2 42.3 %copy-start.1 = (f32[8,32,512]{2,1,0:T(8,128)S(1)}, f32[8,32,512]{2,1,0:T(8,128)}, u32[]{:S(2)}) copy-start(f32[8,32,512]{2,1,0:T(8,128)} %param.8) | copy-start | bytes 1572868
  7.2 299.1 %all-gather.4.cloned.1.call-start = ((), (), s32[]{:S(2)}) async-start(), calls=%async_computation.1 | async-start | bytes 4259840 | tf_op jit(solution)/shard_map/all_gather | solution.py:56
  7.2 25.0 %collective-permute-start = (f32[1,32,512]{2,1,0:T(8,128)S(1)}, f32[1,32,512]{2,1,0:T(8,128)S(1)}, u32[]{:S(2)}, u32[]{:S(2)}) collective-permute-start(f32[1,32,512]{2,1,0:T(8,128)S(1)} %broadcast.45), channel_id=1, source_target_pairs={{16,0},{32,16},{48,32},{64,48},{80,64},{96,80},{112,96},{128,112},... | collective-permute-start | bytes 196616 | tf_op jit(solution)/shard_map/ppermute | solution.py:18
  23.1 16.7 %collective-permute-start.1 = (f32[1,32,512]{2,1,0:T(8,128)S(1)}, f32[1,32,512]{2,1,0:T(8,128)S(1)}, u32[]{:S(2)}, u32[]{:S(2)}) collective-permute-start(f32[1,32,512]{2,1,0:T(8,128)S(1)} %broadcast.45), channel_id=1, source_target_pairs={{0,16},{16,32},{32,48},{48,64},{64,80},{80,96},{96,112},{112,128},... | collective-permute-start | bytes 196616 | tf_op jit(solution)/shard_map/ppermute | solution.py:15
  25.7 23.8 %collective-permute-start.4 = (f32[8,32,32]{2,1,0:T(8,128)}, f32[8,32,32]{2,1,0:T(8,128)}, u32[]{:S(2)}, u32[]{:S(2)}) collective-permute-start(f32[8,32,32]{2,1,0:T(8,128)} %broadcast.46), channel_id=1, source_target_pairs={{2,0},{4,2},{6,4},{8,6},{10,8},{12,10},{14,12},{3,1},{5,3},{7,5},{... | collective-permute-start | bytes 98312 | tf_op jit(solution)/shard_map/ppermute | solution.py:18
  27.0 22.5 %collective-permute-start.5 = (f32[8,32,32]{2,1,0:T(8,128)}, f32[8,32,32]{2,1,0:T(8,128)}, u32[]{:S(2)}, u32[]{:S(2)}) collective-permute-start(f32[8,32,32]{2,1,0:T(8,128)} %broadcast.46), channel_id=1, source_target_pairs={{0,2},{2,4},{4,6},{6,8},{8,10},{10,12},{12,14},{1,3},{3,5},{5,7},{... | collective-permute-start | bytes 98312 | tf_op jit(solution)/shard_map/ppermute | solution.py:15
  39.9 5.3 %copy-start.5 = (f32[8,32,512]{2,1,0:T(8,128)}, f32[8,32,512]{2,1,0:T(8,128)S(1)}, u32[]{:S(2)}) copy-start(f32[8,32,512]{2,1,0:T(8,128)S(1)} %broadcast_in_dim.8) | copy-start | bytes 1572868
  39.9 9.6 %collective-permute-start.2 = (f32[10,1,512]{2,1,0:T(1,128)S(1)}, f32[10,1,512]{2,1,0:T(1,128)S(1)}, u32[]{:S(2)}, u32[]{:S(2)}) collective-permute-start(f32[10,1,512]{2,1,0:T(1,128)S(1)} %get-tuple-element.8), channel_id=1, source_target_pairs={{1,0},{3,2},{5,4},{7,6},{9,8},{11,10},{13,12},{15,14},{17,16},{19,... | collective-permute-start | bytes 61448 | tf_op jit(solution)/shard_map/ppermute | solution.py:18
  41.2 8.3 %collective-permute-start.3 = (f32[10,1,512]{2,1,0:T(1,128)S(1)}, f32[10,1,512]{2,1,0:T(1,128)S(1)}, u32[]{:S(2)}, u32[]{:S(2)}) collective-permute-start(f32[10,1,512]{2,1,0:T(1,128)S(1)} %get-tuple-element.9), channel_id=1, source_target_pairs={{0,1},{2,3},{4,5},{6,7},{8,9},{10,11},{12,13},{14,15},{16,17},{18,... | collective-permute-start | bytes 61448 | tf_op jit(solution)/shard_map/ppermute | solution.py:15
  51.2 23.4 %copy-start.4 = (f32[8,32,512]{2,1,0:T(8,128)}, f32[8,32,512]{2,1,0:T(8,128)S(1)}, u32[]{:S(2)}) copy-start(f32[8,32,512]{2,1,0:T(8,128)S(1)} %fusion.14) | copy-start | bytes 1572868
  51.2 23.4 %collective-permute-start.6 = (f32[1,32,512]{2,1,0:T(8,128)S(1)}, f32[1,32,512]{2,1,0:T(8,128)S(1)}, u32[]{:S(2)}, u32[]{:S(2)}) collective-permute-start(f32[1,32,512]{2,1,0:T(8,128)S(1)} %get-tuple-element.19), channel_id=1, source_target_pairs={{16,0},{32,16},{48,32},{64,48},{80,64},{96,80},{112,96},{128,112},... | collective-permute-start | bytes 196616 | tf_op jit(solution)/shard_map/ppermute | solution.py:18
  57.1 17.5 %collective-permute-start.7 = (f32[1,32,512]{2,1,0:T(8,128)S(1)}, f32[1,32,512]{2,1,0:T(8,128)S(1)}, u32[]{:S(2)}, u32[]{:S(2)}) collective-permute-start(f32[1,32,512]{2,1,0:T(8,128)S(1)} %get-tuple-element.18), channel_id=1, source_target_pairs={{0,16},{16,32},{32,48},{48,64},{64,80},{80,96},{96,112},{112,128},... | collective-permute-start | bytes 196616 | tf_op jit(solution)/shard_map/ppermute | solution.py:15
  66.5 19.2 %collective-permute-start.10 = (f32[8,32,32]{2,1,0:T(8,128)}, f32[8,32,32]{2,1,0:T(8,128)S(1)}, u32[]{:S(2)}, u32[]{:S(2)}) collective-permute-start(f32[8,32,32]{2,1,0:T(8,128)} %get-tuple-element.20), channel_id=1, source_target_pairs={{2,0},{4,2},{6,4},{8,6},{10,8},{12,10},{14,12},{3,1},{5,3},{7,5},{... | collective-permute-start | bytes 98312 | tf_op jit(solution)/shard_map/ppermute | solution.py:18
  67.8 18.0 %collective-permute-start.11 = (f32[8,32,32]{2,1,0:T(8,128)}, f32[8,32,32]{2,1,0:T(8,128)S(1)}, u32[]{:S(2)}, u32[]{:S(2)}) collective-permute-start(f32[8,32,32]{2,1,0:T(8,128)} %get-tuple-element.21), channel_id=1, source_target_pairs={{0,2},{2,4},{4,6},{6,8},{8,10},{10,12},{12,14},{1,3},{3,5},{5,7},{... | collective-permute-start | bytes 98312 | tf_op jit(solution)/shard_map/ppermute | solution.py:15
  75.2 10.5 %collective-permute-start.8 = (f32[10,1,512]{2,1,0:T(1,128)}, f32[10,1,512]{2,1,0:T(1,128)}, u32[]{:S(2)}, u32[]{:S(2)}) collective-permute-start(f32[10,1,512]{2,1,0:T(1,128)} %get-tuple-element.6), channel_id=1, source_target_pairs={{1,0},{3,2},{5,4},{7,6},{9,8},{11,10},{13,12},{15,14},{17,16},{19,... | collective-permute-start | bytes 61448 | tf_op jit(solution)/shard_map/ppermute | solution.py:18
  76.5 9.3 %collective-permute-start.9 = (f32[10,1,512]{2,1,0:T(1,128)}, f32[10,1,512]{2,1,0:T(1,128)}, u32[]{:S(2)}, u32[]{:S(2)}) collective-permute-start(f32[10,1,512]{2,1,0:T(1,128)} %get-tuple-element.7), channel_id=1, source_target_pairs={{0,1},{2,3},{4,5},{6,7},{8,9},{10,11},{12,13},{14,15},{16,17},{18,... | collective-permute-start | bytes 61448 | tf_op jit(solution)/shard_map/ppermute | solution.py:15
  88.7 23.0 %copy-start.3 = (f32[8,32,512]{2,1,0:T(8,128)}, f32[8,32,512]{2,1,0:T(8,128)S(1)}, u32[]{:S(2)}) copy-start(f32[8,32,512]{2,1,0:T(8,128)S(1)} %fusion.31) | copy-start | bytes 1572868
  88.7 83.6 %copy-start.6 = (s32[1,1,1,7]{3,2,1,0:T(1,128)S(1)}, s32[1,1,1,7]{3,2,1,0:T(1,128)}, u32[]{:S(2)}) copy-start(s32[1,1,1,7]{3,2,1,0:T(1,128)} %param.12) | copy-start | bytes 88
  88.7 22.9 %collective-permute-start.12 = (f32[1,32,512]{2,1,0:T(8,128)S(1)}, f32[1,32,512]{2,1,0:T(8,128)S(1)}, u32[]{:S(2)}, u32[]{:S(2)}) collective-permute-start(f32[1,32,512]{2,1,0:T(8,128)S(1)} %get-tuple-element.15), channel_id=1, source_target_pairs={{16,0},{32,16},{48,32},{64,48},{80,64},{96,80},{112,96},{128,112},... | collective-permute-start | bytes 196616 | tf_op jit(solution)/shard_map/ppermute | solution.py:18
  93.3 18.3 %collective-permute-start.13 = (f32[1,32,512]{2,1,0:T(8,128)S(1)}, f32[1,32,512]{2,1,0:T(8,128)S(1)}, u32[]{:S(2)}, u32[]{:S(2)}) collective-permute-start(f32[1,32,512]{2,1,0:T(8,128)S(1)} %get-tuple-element.14), channel_id=1, source_target_pairs={{0,16},{16,32},{32,48},{48,64},{64,80},{80,96},{96,112},{112,128},... | collective-permute-start | bytes 196616 | tf_op jit(solution)/shard_map/ppermute | solution.py:15
  104.0 13.8 %collective-permute-start.16 = (f32[8,32,32]{2,1,0:T(8,128)}, f32[8,32,32]{2,1,0:T(8,128)S(1)}, u32[]{:S(2)}, u32[]{:S(2)}) collective-permute-start(f32[8,32,32]{2,1,0:T(8,128)} %get-tuple-element.16), channel_id=1, source_target_pairs={{2,0},{4,2},{6,4},{8,6},{10,8},{12,10},{14,12},{3,1},{5,3},{7,5},{... | collective-permute-start | bytes 98312 | tf_op jit(solution)/shard_map/ppermute | solution.py:18
  105.3 12.5 %collective-permute-start.17 = (f32[8,32,32]{2,1,0:T(8,128)}, f32[8,32,32]{2,1,0:T(8,128)S(1)}, u32[]{:S(2)}, u32[]{:S(2)}) collective-permute-start(f32[8,32,32]{2,1,0:T(8,128)} %get-tuple-element.17), channel_id=1, source_target_pairs={{0,2},{2,4},{4,6},{6,8},{8,10},{10,12},{12,14},{1,3},{3,5},{5,7},{... | collective-permute-start | bytes 98312 | tf_op jit(solution)/shard_map/ppermute | solution.py:15
  112.3 5.5 %collective-permute-start.14 = (f32[10,1,512]{2,1,0:T(1,128)}, f32[10,1,512]{2,1,0:T(1,128)}, u32[]{:S(2)}, u32[]{:S(2)}) collective-permute-start(f32[10,1,512]{2,1,0:T(1,128)} %get-tuple-element.4), channel_id=1, source_target_pairs={{1,0},{3,2},{5,4},{7,6},{9,8},{11,10},{13,12},{15,14},{17,16},{19,... | collective-permute-start | bytes 61448 | tf_op jit(solution)/shard_map/ppermute | solution.py:18
  113.6 4.8 %collective-permute-start.15 = (f32[10,1,512]{2,1,0:T(1,128)}, f32[10,1,512]{2,1,0:T(1,128)}, u32[]{:S(2)}, u32[]{:S(2)}) collective-permute-start(f32[10,1,512]{2,1,0:T(1,128)} %get-tuple-element.5), channel_id=1, source_target_pairs={{0,1},{2,3},{4,5},{6,7},{8,9},{10,11},{12,13},{14,15},{16,17},{18,... | collective-permute-start | bytes 61448 | tf_op jit(solution)/shard_map/ppermute | solution.py:15
  121.3 0.8 copy-start.2
  171.6 258.1 %all-reduce.6.cloned.1.call-start = ((), (), s32[]{:S(2)}) async-start(), calls=%async_computation | async-start | bytes 262144 | tf_op jit(solution)/shard_map/psum | solution.py:81
  173.9 151.5 %collective-permute-start.18 = (f32[1,32,512]{2,1,0:T(8,128)}, f32[1,32,512]{2,1,0:T(8,128)S(1)}, u32[]{:S(2)}, u32[]{:S(2)}) collective-permute-start(f32[1,32,512]{2,1,0:T(8,128)} %get-tuple-element.11), channel_id=1, source_target_pairs={{16,0},{32,16},{48,32},{64,48},{80,64},{96,80},{112,96},{128,112},... | collective-permute-start | bytes 196616 | tf_op jit(solution)/shard_map/ppermute | solution.py:18
  177.6 147.8 %collective-permute-start.19 = (f32[1,32,512]{2,1,0:T(8,128)}, f32[1,32,512]{2,1,0:T(8,128)S(1)}, u32[]{:S(2)}, u32[]{:S(2)}) collective-permute-start(f32[1,32,512]{2,1,0:T(8,128)} %get-tuple-element.10), channel_id=1, source_target_pairs={{0,16},{16,32},{32,48},{48,64},{64,80},{80,96},{96,112},{112,128},... | collective-permute-start | bytes 196616 | tf_op jit(solution)/shard_map/ppermute | solution.py:15
  318.9 119.4 %collective-permute-start.22 = (f32[8,32,32]{2,1,0:T(8,128)}, f32[8,32,32]{2,1,0:T(8,128)S(1)}, u32[]{:S(2)}, u32[]{:S(2)}) collective-permute-start(f32[8,32,32]{2,1,0:T(8,128)} %get-tuple-element.12), channel_id=1, source_target_pairs={{2,0},{4,2},{6,4},{8,6},{10,8},{12,10},{14,12},{3,1},{5,3},{7,5},{... | collective-permute-start | bytes 98312 | tf_op jit(solution)/shard_map/ppermute | solution.py:18
  320.2 118.1 %collective-permute-start.23 = (f32[8,32,32]{2,1,0:T(8,128)}, f32[8,32,32]{2,1,0:T(8,128)}, u32[]{:S(2)}, u32[]{:S(2)}) collective-permute-start(f32[8,32,32]{2,1,0:T(8,128)} %get-tuple-element.13), channel_id=1, source_target_pairs={{0,2},{2,4},{4,6},{6,8},{8,10},{10,12},{12,14},{1,3},{3,5},{5,7},{... | collective-permute-start | bytes 98312 | tf_op jit(solution)/shard_map/ppermute | solution.py:15
  327.0 111.2 %collective-permute-start.20 = (f32[10,1,512]{2,1,0:T(1,128)}, f32[10,1,512]{2,1,0:T(1,128)S(1)}, u32[]{:S(2)}, u32[]{:S(2)}) collective-permute-start(f32[10,1,512]{2,1,0:T(1,128)} %get-tuple-element.2), channel_id=1, source_target_pairs={{1,0},{3,2},{5,4},{7,6},{9,8},{11,10},{13,12},{15,14},{17,16},{19,... | collective-permute-start | bytes 61448 | tf_op jit(solution)/shard_map/ppermute | solution.py:18
  328.3 110.0 %collective-permute-start.21 = (f32[10,1,512]{2,1,0:T(1,128)}, f32[10,1,512]{2,1,0:T(1,128)S(1)}, u32[]{:S(2)}, u32[]{:S(2)}) collective-permute-start(f32[10,1,512]{2,1,0:T(1,128)} %get-tuple-element.3), channel_id=1, source_target_pairs={{0,1},{2,3},{4,5},{6,7},{8,9},{10,11},{12,13},{14,15},{16,17},{18,... | collective-permute-start | bytes 61448 | tf_op jit(solution)/shard_map/ppermute | solution.py:15
Sparse Core Ops, SparseCore 0:
  171.7 134.5 all-gather.3
  317.3 112.3 all-reduce.5
where the time goes:
time: 450 us; the launch traced here: 449 us
  waiting for transfers between devices  224 us (50%)
  starting transfers between devices  110 us (24%)
  blocking collectives  42.9 us (10%)
  local copies, waits for them, and re-layouts  30.8 us (7%)
  other arithmetic  16.1 us (4%)
  between operations  15.2 us (3%)
  matrix products  9.88 us (2%)
    all_gather x1, waiting for transfers between devices, body(): piece = lax.all_gather(block_traces[None], ('gx', 'gz'), axis=0, tiled=True)  118 us
    psum x1, waiting for transfers between devices, body(): total = lax.psum(partial_rows, 'gy')  98.3 us
    ppermute x12, starting transfers between devices, extended(): lax.ppermute(lax.slice_in_dim(block, block.shape[dim] - width, None, axis...  69.5 us
    all_gather x1, blocking collectives, body(): face_block = lax.all_gather(face_local, 'gy', axis=1, tiled=True)  42.9 us
    ppermute x12, starting transfers between devices, extended(): lax.ppermute(lax.slice_in_dim(block, 0, width, axis=dim), axis, backward)  40.3 us
    div x4, other arithmetic, sweep(): return (rhs + beside) / diag  11.1 us
  transfers between devices with their start and end apart: 26, of which 4 were waited for; matrix products, arithmetic and copies ran while one was open for 8% of the time, Pallas kernels for 0%

commit v1 on v0

--- a/solution.py
+++ b/solution.py
@@ -5,6 +5,12 @@
 
 E = 32
 SWEEPS = 3
+
+
+def summed_here(x, axis):
+    shards = lax.all_gather(x, axis, axis=0, tiled=False)
+    total = shards.sum(axis=0)
+    return total
 
 
 def extended(block, sides, width):
@@ -78,7 +84,7 @@
         preferred_element_type=jnp.float32,
     )
     partial_rows = nearpart + farpart
-    total = lax.psum(partial_rows, "gy")
+    total = summed_here(partial_rows, "gy")
     face_flux = total[:, perm].reshape(E, rows_x, cells_y * groups)
     mine = lax.dynamic_slice_in_dim(face_flux, mine_y * cells_y, cells_y, 2)
     flux_rows = mine.transpose(1, 2, 0).reshape(rows_x, cells_y * E)

time: 450 us -> 399 us (0.89)
  the two profiles are of different devices: /device:TPU:2 before, /device:TPU:6 now
where the time goes in v1:
time: 399 us; the launch traced here: 398 us
  waiting for transfers between devices  172 us (43%)
  starting transfers between devices  112 us (28%)
  blocking collectives  42.8 us (11%)
  local copies, waits for them, and re-layouts  29.2 us (7%)
  other arithmetic  17.3 us (4%)
  between operations  15.2 us (4%)
  matrix products  9.77 us (2%)
    all_gather x1, waiting for transfers between devices, body(): piece = lax.all_gather(block_traces[None], ('gx', 'gz'), axis=0, tiled=True)  129 us
    ppermute x12, starting transfers between devices, extended(): lax.ppermute(lax.slice_in_dim(block, block.shape[dim] - width, None, axis...  68.8 us
    all_gather x1, blocking collectives, body(): face_block = lax.all_gather(face_local, 'gy', axis=1, tiled=True)  42.8 us
    ppermute x12, starting transfers between devices, extended(): lax.ppermute(lax.slice_in_dim(block, 0, width, axis=dim), axis, backward)  42.7 us
    all_gather x1, waiting for transfers between devices, summed_here(): shards = lax.all_gather(x, axis, axis=0, tiled=False)  29.8 us
    ppermute x12, waiting for transfers between devices, extended(): lax.ppermute(lax.slice_in_dim(block, block.shape[dim] - width, None, axis...  12.7 us
    div x4, other arithmetic, sweep(): return (rhs + beside) / diag  11 us
  transfers between devices with their start and end apart: 26, of which 7 were waited for; matrix products, arithmetic and copies ran while one was open for 7% of the time, Pallas kernels for 0%

profile of v1, /device:TPU:6, one launch (start us, length us, event | category | flops | bytes accessed | tf_op | source)
XLA Modules:
  0.0 397.9 jit_solution(9854299509466809790)
XLA Ops:
  7.2 16.1 %collective-permute-start = (f32[1,32,512]{2,1,0:T(8,128)S(1)}, f32[1,32,512]{2,1,0:T(8,128)S(1)}, u32[]{:S(2)}, u32[]{:S(2)}) collective-permute-start(f32[1,32,512]{2,1,0:T(8,128)S(1)} %broadcast.45), channel_id=1, source_target_pairs={{16,0},{32,16},{48,32},{64,48},{80,64},{96,80},{112,96},{128,112},... | collective-permute-start | bytes 196616 | tf_op jit(solution)/shard_map/ppermute | solution.py:24
  23.4 1.9 collective-permute-start.1
  26.0 1.3 collective-permute-start.4
  27.3 5.2 %collective-permute-start.5 = (f32[8,32,32]{2,1,0:T(8,128)}, f32[8,32,32]{2,1,0:T(8,128)}, u32[]{:S(2)}, u32[]{:S(2)}) collective-permute-start(f32[8,32,32]{2,1,0:T(8,128)} %broadcast.46), channel_id=1, source_target_pairs={{0,2},{2,4},{4,6},{6,8},{8,10},{10,12},{12,14},{1,3},{3,5},{5,7},{... | collective-permute-start | bytes 98312 | tf_op jit(solution)/shard_map/ppermute | solution.py:21
  32.5 7.2 %collective-permute-done.1 = f32[1,32,512]{2,1,0:T(8,128)S(1)} collective-permute-done((f32[1,32,512]{2,1,0:T(8,128)S(1)}, f32[1,32,512]{2,1,0:T(8,128)S(1)}, u32[]{:S(2)}, u32[]{:S(2)}) %collective-permute-start.1) | collective-permute-done | bytes 65568 | tf_op jit(solution)/shard_map/ppermute | solution.py:21
  39.7 1.3 collective-permute-start.2
  41.0 3.0 collective-permute-start.3
  45.0 2.0 broadcast_in_dim.18
  47.0 2.3 reshape.71
  49.4 1.6 fusion.14
  51.0 6.4 %collective-permute-start.6 = (f32[1,32,512]{2,1,0:T(8,128)S(1)}, f32[1,32,512]{2,1,0:T(8,128)S(1)}, u32[]{:S(2)}, u32[]{:S(2)}) collective-permute-start(f32[1,32,512]{2,1,0:T(8,128)S(1)} %get-tuple-element.19), channel_id=1, source_target_pairs={{16,0},{32,16},{48,32},{64,48},{80,64},{96,80},{112,96},{128,112},... | collective-permute-start | bytes 196616 | tf_op jit(solution)/shard_map/ppermute | solution.py:24
  57.4 8.2 %collective-permute-start.7 = (f32[1,32,512]{2,1,0:T(8,128)S(1)}, f32[1,32,512]{2,1,0:T(8,128)S(1)}, u32[]{:S(2)}, u32[]{:S(2)}) collective-permute-start(f32[1,32,512]{2,1,0:T(8,128)S(1)} %get-tuple-element.18), channel_id=1, source_target_pairs={{0,16},{16,32},{32,48},{48,64},{64,80},{80,96},{96,112},{112,128},... | collective-permute-start | bytes 196616 | tf_op jit(solution)/shard_map/ppermute | solution.py:21
  66.4 1.3 collective-permute-start.10
  67.6 6.0 %collective-permute-start.11 = (f32[8,32,32]{2,1,0:T(8,128)}, f32[8,32,32]{2,1,0:T(8,128)S(1)}, u32[]{:S(2)}, u32[]{:S(2)}) collective-permute-start(f32[8,32,32]{2,1,0:T(8,128)} %get-tuple-element.21), channel_id=1, source_target_pairs={{0,2},{2,4},{4,6},{6,8},{8,10},{10,12},{12,14},{1,3},{3,5},{5,7},{... | collective-permute-start | bytes 98312 | tf_op jit(solution)/shard_map/ppermute | solution.py:21
  73.7 1.4 collective-permute-done.7
  75.8 1.3 collective-permute-start.8
  77.1 4.2 %collective-permute-start.9 = (f32[10,1,512]{2,1,0:T(1,128)}, f32[10,1,512]{2,1,0:T(1,128)}, u32[]{:S(2)}, u32[]{:S(2)}) collective-permute-start(f32[10,1,512]{2,1,0:T(1,128)} %get-tuple-element.7), channel_id=1, source_target_pairs={{0,1},{2,3},{4,5},{6,7},{8,9},{10,11},{12,13},{14,15},{16,17},{18,... | collective-permute-start | bytes 61448 | tf_op jit(solution)/shard_map/ppermute | solution.py:21
  82.0 4.3 %scatter_custom_fusion = s32[1024]{0:T(1024)S(1)} fusion(s32[1024]{0:T(1024)S(1)} %bitcast.40, s32[1024]{0:T(1024)S(1)} %iota.13, s32[]{:T(128)} %constant.10.clone.1), kind=kCustom, calls=%fused_computation.106 | custom fusion | bytes 4100 | tf_op jit(solution)/shard_map/scatter | solution.py:59
  86.3 2.9 fusion.31
  89.2 8.1 %collective-permute-start.12 = (f32[1,32,512]{2,1,0:T(8,128)S(1)}, f32[1,32,512]{2,1,0:T(8,128)S(1)}, u32[]{:S(2)}, u32[]{:S(2)}) collective-permute-start(f32[1,32,512]{2,1,0:T(8,128)S(1)} %get-tuple-element.15), channel_id=1, source_target_pairs={{16,0},{32,16},{48,32},{64,48},{80,64},{96,80},{112,96},{128,112},... | collective-permute-start | bytes 196616 | tf_op jit(solution)/shard_map/ppermute | solution.py:24
  97.3 6.5 %collective-permute-start.13 = (f32[1,32,512]{2,1,0:T(8,128)S(1)}, f32[1,32,512]{2,1,0:T(8,128)S(1)}, u32[]{:S(2)}, u32[]{:S(2)}) collective-permute-start(f32[1,32,512]{2,1,0:T(8,128)S(1)} %get-tuple-element.14), channel_id=1, source_target_pairs={{0,16},{16,32},{32,48},{48,64},{64,80},{80,96},{96,112},{112,128},... | collective-permute-start | bytes 196616 | tf_op jit(solution)/shard_map/ppermute | solution.py:21
  104.6 1.3 collective-permute-start.16
  105.9 7.5 %collective-permute-start.17 = (f32[8,32,32]{2,1,0:T(8,128)}, f32[8,32,32]{2,1,0:T(8,128)S(1)}, u32[]{:S(2)}, u32[]{:S(2)}) collective-permute-start(f32[8,32,32]{2,1,0:T(8,128)} %get-tuple-element.17), channel_id=1, source_target_pairs={{0,2},{2,4},{4,6},{6,8},{8,10},{10,12},{12,14},{1,3},{3,5},{5,7},{... | collective-permute-start | bytes 98312 | tf_op jit(solution)/shard_map/ppermute | solution.py:21
  113.4 2.3 collective-permute-done.13
  116.3 1.3 collective-permute-start.14
  117.6 4.2 %collective-permute-start.15 = (f32[10,1,512]{2,1,0:T(1,128)}, f32[10,1,512]{2,1,0:T(1,128)}, u32[]{:S(2)}, u32[]{:S(2)}) collective-permute-start(f32[10,1,512]{2,1,0:T(1,128)} %get-tuple-element.5), channel_id=1, source_target_pairs={{0,1},{2,3},{4,5},{6,7},{8,9},{10,11},{12,13},{14,15},{16,17},{18,... | collective-permute-start | bytes 61448 | tf_op jit(solution)/shard_map/ppermute | solution.py:21
  122.4 2.8 fusion.24
  126.1 42.8 %all-gather = bf16[8,1,4096]{2,1,0:T(2,128)(2,1)S(1)} all-gather(bf16[8,1,512]{2,1,0:T(2,128)(2,1)S(1)} %fusion.43), channel_id=2, replica_groups=mesh['gx'=32,'gy'=8,'gz'=2] {'gy'}, dimensions={2}, use_global_device_ids=true | all-gather | bytes 73728 | tf_op jit(solution)/shard_map/all_gather | solution.py:57
  169.4 4.3 %gather_fusion = bf16[1024,32]{1,0:T(8,128)(2,1)} fusion(bf16[1024,32]{1,0:T(8,128)(2,1)S(1)} %reshape.72, s32[1024]{0:T(1024)S(1)} %fusion.44), kind=kCustom, calls=%fused_computation | custom fusion | bytes 135168 | tf_op jit(solution)/shard_map/gather | solution.py:60
  173.7 1.7 copy.15
  176.4 129.2 %all-gather.6.cloned.1.call-done = bf16[2048,1024]{1,0:T(8,128)(2,1)} async-done(((bf16[32,1024]{1,0:T(8,128)(2,1)}), bf16[2048,1024]{1,0:T(8,128)(2,1)}) %all-gather.6.cloned.1.call-update) | async-done | bytes 4194320 | tf_op jit(solution)/shard_map/all_gather | solution.py:62
  305.6 6.7 %fusion.4 = bf16[8,32,1024]{2,0,1:T(8,128)(2,1)S(1)} fusion(bf16[64,32,1024]{2,1,0:T(8,128)(2,1)} %bitcast.36, s32[8]{0:T(128)S(1)} %pad_add_fusion), kind=kOutput, calls=%fused_computation.7 | convolution fusion | flops 33817088 | bytes 4718624 | tf_op jit(solution)/shard_map/cn,net->cet/dot_general | solution.py:65
  312.2 0.9 slice.231
  314.0 2.4 fusion.7
  317.3 1.9 collective-permute-start.18
  319.3 12.6 %collective-permute-start.19 = (f32[1,32,512]{2,1,0:T(8,128)S(1)}, f32[1,32,512]{2,1,0:T(8,128)S(1)}, u32[]{:S(2)}, u32[]{:S(2)}) collective-permute-start(f32[1,32,512]{2,1,0:T(8,128)S(1)} %get-tuple-element.10), channel_id=1, source_target_pairs={{0,16},{16,32},{32,48},{48,64},{64,80},{80,96},{96,112},{112,128},... | collective-permute-start | bytes 196616 | tf_op jit(solution)/shard_map/ppermute | solution.py:21
  331.9 1.7 fusion.51
  333.6 1.3 collective-permute-start.22
  334.9 5.2 %collective-permute-start.23 = (f32[8,32,32]{2,1,0:T(8,128)}, f32[8,32,32]{2,1,0:T(8,128)}, u32[]{:S(2)}, u32[]{:S(2)}) collective-permute-start(f32[8,32,32]{2,1,0:T(8,128)} %get-tuple-element.13), channel_id=1, source_target_pairs={{0,2},{2,4},{4,6},{6,8},{8,10},{10,12},{12,14},{1,3},{3,5},{5,7},{... | collective-permute-start | bytes 98312 | tf_op jit(solution)/shard_map/ppermute | solution.py:21
  340.1 1.3 collective-permute-done.19
  341.4 1.6 pad_maximum_fusion.38
  343.1 1.3 collective-permute-start.20
  344.3 4.2 %collective-permute-start.21 = (f32[10,1,512]{2,1,0:T(1,128)}, f32[10,1,512]{2,1,0:T(1,128)}, u32[]{:S(2)}, u32[]{:S(2)}) collective-permute-start(f32[10,1,512]{2,1,0:T(1,128)} %get-tuple-element.3), channel_id=1, source_target_pairs={{0,1},{2,3},{4,5},{6,7},{8,9},{10,11},{12,13},{14,15},{16,17},{18,... | collective-permute-start | bytes 61448 | tf_op jit(solution)/shard_map/ppermute | solution.py:21
  348.6 29.8 %all-gather.8.cloned.1.call-done = f32[256,1024]{1,0:T(8,128)} async-done(((f32[32,1024]{1,0:T(8,128)}), f32[256,1024]{1,0:T(8,128)}) %all-gather.8.cloned.1.call-update) | async-done | bytes 1048592 | tf_op jit(solution)/shard_map/all_gather | solution.py:11
  378.4 1.3 reduce_sum.9
  379.7 1.0 copy.18
  380.7 5.1 %gather_fusion.1 = f32[1024,32]{1,0:T(8,128)} fusion(f32[32,1024]{0,1:T(8,128)} %copy.18, s32[1024]{0:T(1024)S(1)} %broadcast_clamp_fusion), kind=kCustom, calls=%fused_computation.1 | custom fusion | bytes 266240 | tf_op jit(solution)/shard_map/gather | solution.py:88
  387.4 3.7 fusion.17
  (67 shorter events, 11.0 us)
Async XLA Ops:
  7.2 306.1 %copy-start = (bf16[1,1,1,1024,1024]{4,3,2,1,0:T(8,128)(2,1)S(1)}, bf16[1,1,1,1024,1024]{4,3,2,1,0:T(8,128)(2,1)}, u32[]{:S(2)}) copy-start(bf16[1,1,1,1024,1024]{4,3,2,1,0:T(8,128)(2,1)} %param.13) | copy-start | bytes 6291460
  7.2 42.2 %copy-start.1 = (f32[8,32,512]{2,1,0:T(8,128)S(1)}, f32[8,32,512]{2,1,0:T(8,128)}, u32[]{:S(2)}) copy-start(f32[8,32,512]{2,1,0:T(8,128)} %param.8) | copy-start | bytes 1572868
  7.2 298.4 %all-gather.6.cloned.1.call-start = ((), (), s32[]{:S(2)}) async-start(), calls=%async_computation | async-start | bytes 4259840 | tf_op jit(solution)/shard_map/all_gather | solution.py:62
  7.2 25.2 %collective-permute-start = (f32[1,32,512]{2,1,0:T(8,128)S(1)}, f32[1,32,512]{2,1,0:T(8,128)S(1)}, u32[]{:S(2)}, u32[]{:S(2)}) collective-permute-start(f32[1,32,512]{2,1,0:T(8,128)S(1)} %broadcast.45), channel_id=1, source_target_pairs={{16,0},{32,16},{48,32},{64,48},{80,64},{96,80},{112,96},{128,112},... | collective-permute-start | bytes 196616 | tf_op jit(solution)/shard_map/ppermute | solution.py:24
  23.4 16.3 %collective-permute-start.1 = (f32[1,32,512]{2,1,0:T(8,128)S(1)}, f32[1,32,512]{2,1,0:T(8,128)S(1)}, u32[]{:S(2)}, u32[]{:S(2)}) collective-permute-start(f32[1,32,512]{2,1,0:T(8,128)S(1)} %broadcast.45), channel_id=1, source_target_pairs={{0,16},{16,32},{32,48},{48,64},{64,80},{80,96},{96,112},{112,128},... | collective-permute-start | bytes 196616 | tf_op jit(solution)/shard_map/ppermute | solution.py:21
  26.0 23.3 %collective-permute-start.4 = (f32[8,32,32]{2,1,0:T(8,128)}, f32[8,32,32]{2,1,0:T(8,128)}, u32[]{:S(2)}, u32[]{:S(2)}) collective-permute-start(f32[8,32,32]{2,1,0:T(8,128)} %broadcast.46), channel_id=1, source_target_pairs={{2,0},{4,2},{6,4},{8,6},{10,8},{12,10},{14,12},{3,1},{5,3},{7,5},{... | collective-permute-start | bytes 98312 | tf_op jit(solution)/shard_map/ppermute | solution.py:24
  27.3 22.1 %collective-permute-start.5 = (f32[8,32,32]{2,1,0:T(8,128)}, f32[8,32,32]{2,1,0:T(8,128)}, u32[]{:S(2)}, u32[]{:S(2)}) collective-permute-start(f32[8,32,32]{2,1,0:T(8,128)} %broadcast.46), channel_id=1, source_target_pairs={{0,2},{2,4},{4,6},{6,8},{8,10},{10,12},{12,14},{1,3},{3,5},{5,7},{... | collective-permute-start | bytes 98312 | tf_op jit(solution)/shard_map/ppermute | solution.py:21
  39.7 5.3 %copy-start.5 = (f32[8,32,512]{2,1,0:T(8,128)}, f32[8,32,512]{2,1,0:T(8,128)S(1)}, u32[]{:S(2)}) copy-start(f32[8,32,512]{2,1,0:T(8,128)S(1)} %broadcast_in_dim.8) | copy-start | bytes 1572868
  39.7 9.6 %collective-permute-start.2 = (f32[10,1,512]{2,1,0:T(1,128)S(1)}, f32[10,1,512]{2,1,0:T(1,128)S(1)}, u32[]{:S(2)}, u32[]{:S(2)}) collective-permute-start(f32[10,1,512]{2,1,0:T(1,128)S(1)} %get-tuple-element.8), channel_id=1, source_target_pairs={{1,0},{3,2},{5,4},{7,6},{9,8},{11,10},{13,12},{15,14},{17,16},{19,... | collective-permute-start | bytes 61448 | tf_op jit(solution)/shard_map/ppermute | solution.py:24
  41.0 8.3 %collective-permute-start.3 = (f32[10,1,512]{2,1,0:T(1,128)S(1)}, f32[10,1,512]{2,1,0:T(1,128)S(1)}, u32[]{:S(2)}, u32[]{:S(2)}) collective-permute-start(f32[10,1,512]{2,1,0:T(1,128)S(1)} %get-tuple-element.9), channel_id=1, source_target_pairs={{0,1},{2,3},{4,5},{6,7},{8,9},{10,11},{12,13},{14,15},{16,17},{18,... | collective-permute-start | bytes 61448 | tf_op jit(solution)/shard_map/ppermute | solution.py:21
  51.0 24.1 %copy-start.4 = (f32[8,32,512]{2,1,0:T(8,128)}, f32[8,32,512]{2,1,0:T(8,128)S(1)}, u32[]{:S(2)}) copy-start(f32[8,32,512]{2,1,0:T(8,128)S(1)} %fusion.14) | copy-start | bytes 1572868
  51.0 22.6 %collective-permute-start.6 = (f32[1,32,512]{2,1,0:T(8,128)S(1)}, f32[1,32,512]{2,1,0:T(8,128)S(1)}, u32[]{:S(2)}, u32[]{:S(2)}) collective-permute-start(f32[1,32,512]{2,1,0:T(8,128)S(1)} %get-tuple-element.19), channel_id=1, source_target_pairs={{16,0},{32,16},{48,32},{64,48},{80,64},{96,80},{112,96},{128,112},... | collective-permute-start | bytes 196616 | tf_op jit(solution)/shard_map/ppermute | solution.py:24
  57.4 17.7 %collective-permute-start.7 = (f32[1,32,512]{2,1,0:T(8,128)S(1)}, f32[1,32,512]{2,1,0:T(8,128)S(1)}, u32[]{:S(2)}, u32[]{:S(2)}) collective-permute-start(f32[1,32,512]{2,1,0:T(8,128)S(1)} %get-tuple-element.18), channel_id=1, source_target_pairs={{0,16},{16,32},{32,48},{48,64},{64,80},{80,96},{96,112},{112,128},... | collective-permute-start | bytes 196616 | tf_op jit(solution)/shard_map/ppermute | solution.py:21
  66.4 19.9 %collective-permute-start.10 = (f32[8,32,32]{2,1,0:T(8,128)}, f32[8,32,32]{2,1,0:T(8,128)S(1)}, u32[]{:S(2)}, u32[]{:S(2)}) collective-permute-start(f32[8,32,32]{2,1,0:T(8,128)} %get-tuple-element.20), channel_id=1, source_target_pairs={{2,0},{4,2},{6,4},{8,6},{10,8},{12,10},{14,12},{3,1},{5,3},{7,5},{... | collective-permute-start | bytes 98312 | tf_op jit(solution)/shard_map/ppermute | solution.py:24
  67.6 18.7 %collective-permute-start.11 = (f32[8,32,32]{2,1,0:T(8,128)}, f32[8,32,32]{2,1,0:T(8,128)S(1)}, u32[]{:S(2)}, u32[]{:S(2)}) collective-permute-start(f32[8,32,32]{2,1,0:T(8,128)} %get-tuple-element.21), channel_id=1, source_target_pairs={{0,2},{2,4},{4,6},{6,8},{8,10},{10,12},{12,14},{1,3},{3,5},{5,7},{... | collective-permute-start | bytes 98312 | tf_op jit(solution)/shard_map/ppermute | solution.py:21
  75.8 10.5 %collective-permute-start.8 = (f32[10,1,512]{2,1,0:T(1,128)}, f32[10,1,512]{2,1,0:T(1,128)}, u32[]{:S(2)}, u32[]{:S(2)}) collective-permute-start(f32[10,1,512]{2,1,0:T(1,128)} %get-tuple-element.6), channel_id=1, source_target_pairs={{1,0},{3,2},{5,4},{7,6},{9,8},{11,10},{13,12},{15,14},{17,16},{19,... | collective-permute-start | bytes 61448 | tf_op jit(solution)/shard_map/ppermute | solution.py:24
  77.1 9.3 %collective-permute-start.9 = (f32[10,1,512]{2,1,0:T(1,128)}, f32[10,1,512]{2,1,0:T(1,128)}, u32[]{:S(2)}, u32[]{:S(2)}) collective-permute-start(f32[10,1,512]{2,1,0:T(1,128)} %get-tuple-element.7), channel_id=1, source_target_pairs={{0,1},{2,3},{4,5},{6,7},{8,9},{10,11},{12,13},{14,15},{16,17},{18,... | collective-permute-start | bytes 61448 | tf_op jit(solution)/shard_map/ppermute | solution.py:21
  89.2 26.5 %copy-start.3 = (f32[8,32,512]{2,1,0:T(8,128)}, f32[8,32,512]{2,1,0:T(8,128)S(1)}, u32[]{:S(2)}) copy-start(f32[8,32,512]{2,1,0:T(8,128)S(1)} %fusion.31) | copy-start | bytes 1572868
  89.2 87.1 %copy-start.7 = (s32[1,1,1,7]{3,2,1,0:T(1,128)S(1)}, s32[1,1,1,7]{3,2,1,0:T(1,128)}, u32[]{:S(2)}) copy-start(s32[1,1,1,7]{3,2,1,0:T(1,128)} %param.12) | copy-start | bytes 88
  89.2 24.1 %collective-permute-start.12 = (f32[1,32,512]{2,1,0:T(8,128)S(1)}, f32[1,32,512]{2,1,0:T(8,128)S(1)}, u32[]{:S(2)}, u32[]{:S(2)}) collective-permute-start(f32[1,32,512]{2,1,0:T(8,128)S(1)} %get-tuple-element.15), channel_id=1, source_target_pairs={{16,0},{32,16},{48,32},{64,48},{80,64},{96,80},{112,96},{128,112},... | collective-permute-start | bytes 196616 | tf_op jit(solution)/shard_map/ppermute | solution.py:24
  97.3 18.3 %collective-permute-start.13 = (f32[1,32,512]{2,1,0:T(8,128)S(1)}, f32[1,32,512]{2,1,0:T(8,128)S(1)}, u32[]{:S(2)}, u32[]{:S(2)}) collective-permute-start(f32[1,32,512]{2,1,0:T(8,128)S(1)} %get-tuple-element.14), channel_id=1, source_target_pairs={{0,16},{16,32},{32,48},{48,64},{64,80},{80,96},{96,112},{112,128},... | collective-permute-start | bytes 196616 | tf_op jit(solution)/shard_map/ppermute | solution.py:21
  104.6 17.3 %collective-permute-start.16 = (f32[8,32,32]{2,1,0:T(8,128)}, f32[8,32,32]{2,1,0:T(8,128)S(1)}, u32[]{:S(2)}, u32[]{:S(2)}) collective-permute-start(f32[8,32,32]{2,1,0:T(8,128)} %get-tuple-element.16), channel_id=1, source_target_pairs={{2,0},{4,2},{6,4},{8,6},{10,8},{12,10},{14,12},{3,1},{5,3},{7,5},{... | collective-permute-start | bytes 98312 | tf_op jit(solution)/shard_map/ppermute | solution.py:24
  105.9 16.0 %collective-permute-start.17 = (f32[8,32,32]{2,1,0:T(8,128)}, f32[8,32,32]{2,1,0:T(8,128)S(1)}, u32[]{:S(2)}, u32[]{:S(2)}) collective-permute-start(f32[8,32,32]{2,1,0:T(8,128)} %get-tuple-element.17), channel_id=1, source_target_pairs={{0,2},{2,4},{4,6},{6,8},{8,10},{10,12},{12,14},{1,3},{3,5},{5,7},{... | collective-permute-start | bytes 98312 | tf_op jit(solution)/shard_map/ppermute | solution.py:21
  116.3 5.5 %collective-permute-start.14 = (f32[10,1,512]{2,1,0:T(1,128)}, f32[10,1,512]{2,1,0:T(1,128)}, u32[]{:S(2)}, u32[]{:S(2)}) collective-permute-start(f32[10,1,512]{2,1,0:T(1,128)} %get-tuple-element.4), channel_id=1, source_target_pairs={{1,0},{3,2},{5,4},{7,6},{9,8},{11,10},{13,12},{15,14},{17,16},{19,... | collective-permute-start | bytes 61448 | tf_op jit(solution)/shard_map/ppermute | solution.py:24
  117.6 4.8 %collective-permute-start.15 = (f32[10,1,512]{2,1,0:T(1,128)}, f32[10,1,512]{2,1,0:T(1,128)}, u32[]{:S(2)}, u32[]{:S(2)}) collective-permute-start(f32[10,1,512]{2,1,0:T(1,128)} %get-tuple-element.5), channel_id=1, source_target_pairs={{0,1},{2,3},{4,5},{6,7},{8,9},{10,11},{12,13},{14,15},{16,17},{18,... | collective-permute-start | bytes 61448 | tf_op jit(solution)/shard_map/ppermute | solution.py:21
  125.2 0.8 copy-start.2
  175.4 138.6 %copy-start.6 = (bf16[1,1,1,7,16,1024]{5,4,3,2,1,0:T(8,128)(2,1)S(1)}, bf16[1,1,1,7,16,1024]{5,4,3,2,1,0:T(8,128)(2,1)}, u32[]{:S(2)}) copy-start(bf16[1,1,1,7,16,1024]{5,4,3,2,1,0:T(8,128)(2,1)} %param.14) | copy-start | bytes 688132
  175.4 202.9 %all-gather.8.cloned.1.call-start = ((), (), s32[]{:S(2)}) async-start(), calls=%async_computation.1 | async-start | bytes 1179648 | tf_op jit(solution)/shard_map/all_gather | solution.py:11
  317.3 22.8 %collective-permute-start.18 = (f32[1,32,512]{2,1,0:T(8,128)S(1)}, f32[1,32,512]{2,1,0:T(8,128)S(1)}, u32[]{:S(2)}, u32[]{:S(2)}) collective-permute-start(f32[1,32,512]{2,1,0:T(8,128)S(1)} %get-tuple-element.11), channel_id=1, source_target_pairs={{16,0},{32,16},{48,32},{64,48},{80,64},{96,80},{112,96},{128,112},... | collective-permute-start | bytes 196616 | tf_op jit(solution)/shard_map/ppermute | solution.py:24
  319.3 22.2 %collective-permute-start.19 = (f32[1,32,512]{2,1,0:T(8,128)S(1)}, f32[1,32,512]{2,1,0:T(8,128)S(1)}, u32[]{:S(2)}, u32[]{:S(2)}) collective-permute-start(f32[1,32,512]{2,1,0:T(8,128)S(1)} %get-tuple-element.10), channel_id=1, source_target_pairs={{0,16},{16,32},{32,48},{48,64},{64,80},{80,96},{96,112},{112,128},... | collective-permute-start | bytes 196616 | tf_op jit(solution)/shard_map/ppermute | solution.py:21
  333.6 53.7 %collective-permute-start.22 = (f32[8,32,32]{2,1,0:T(8,128)}, f32[8,32,32]{2,1,0:T(8,128)S(1)}, u32[]{:S(2)}, u32[]{:S(2)}) collective-permute-start(f32[8,32,32]{2,1,0:T(8,128)} %get-tuple-element.12), channel_id=1, source_target_pairs={{2,0},{4,2},{6,4},{8,6},{10,8},{12,10},{14,12},{3,1},{5,3},{7,5},{... | collective-permute-start | bytes 98312 | tf_op jit(solution)/shard_map/ppermute | solution.py:24
  334.9 52.4 %collective-permute-start.23 = (f32[8,32,32]{2,1,0:T(8,128)}, f32[8,32,32]{2,1,0:T(8,128)}, u32[]{:S(2)}, u32[]{:S(2)}) collective-permute-start(f32[8,32,32]{2,1,0:T(8,128)} %get-tuple-element.13), channel_id=1, source_target_pairs={{0,2},{2,4},{4,6},{6,8},{8,10},{10,12},{12,14},{1,3},{3,5},{5,7},{... | collective-permute-start | bytes 98312 | tf_op jit(solution)/shard_map/ppermute | solution.py:21
  343.1 44.3 %collective-permute-start.20 = (f32[10,1,512]{2,1,0:T(1,128)}, f32[10,1,512]{2,1,0:T(1,128)}, u32[]{:S(2)}, u32[]{:S(2)}) collective-permute-start(f32[10,1,512]{2,1,0:T(1,128)} %get-tuple-element.2), channel_id=1, source_target_pairs={{1,0},{3,2},{5,4},{7,6},{9,8},{11,10},{13,12},{15,14},{17,16},{19,... | collective-permute-start | bytes 61448 | tf_op jit(solution)/shard_map/ppermute | solution.py:24
  344.3 43.0 %collective-permute-start.21 = (f32[10,1,512]{2,1,0:T(1,128)}, f32[10,1,512]{2,1,0:T(1,128)}, u32[]{:S(2)}, u32[]{:S(2)}) collective-permute-start(f32[10,1,512]{2,1,0:T(1,128)} %get-tuple-element.3), channel_id=1, source_target_pairs={{0,1},{2,3},{4,5},{6,7},{8,9},{10,11},{12,13},{14,15},{16,17},{18,... | collective-permute-start | bytes 61448 | tf_op jit(solution)/shard_map/ppermute | solution.py:21
Sparse Core Ops, SparseCore 0:
  175.6 129.9 all-gather.5
  316.5 61.8 all-gather.7
